TPU v7x, 256 devices: a whole 4x4x8 slice. The times are simulated.
256 devices in a mesh: dp: 64 (over z, y, core), tensor: 4 (over x).
Axes of the slice: x: 4, y: 4, z: 8, core: 2. Of those that a mesh axis runs over, the one named last changes fastest.
Arguments:
- gradient: float32 [48, 1024, 1024], P(None, 'dp', 'tensor'), may hold values from -90 to 90
- second_moment: float32 [48, 1024, 1024], P(None, 'dp', 'tensor'), may hold values from 0.1 to 1
- owner_table: int32 [48], replicated, may hold values from 0 to 63, as said below
- slot_table: int32 [48], replicated, may hold values from 0 to 1, as said below
- left_stat: float32 [64, 2, 1024, 1024], P('dp', None, 'tensor'), may hold values from -1 to 4
- right_stat: float32 [64, 2, 1024, 1024], P('dp', None, 'tensor'), may hold values from -1 to 4
- left_root: bfloat16 [64, 2, 1024, 1024], P('dp', None, 'tensor'), may hold values from -1 to 4
- right_root: bfloat16 [64, 2, 1024, 1024], P('dp', None, 'tensor'), may hold values from -1 to 4
Outputs:
- update: bfloat16 [48, 1024, 1024], P(None, 'dp', 'tensor')
- new_second: float32 [48, 1024, 1024], P(None, 'dp', 'tensor')
- left_new: float32 [64, 2, 1024, 1024], P('dp', None, 'tensor')
- right_new: float32 [64, 2, 1024, 1024], P('dp', None, 'tensor')
Inputs may be any that keep to these rules, and one draw needn't show every extreme that they name: The pairs (owner_table[b], slot_table[b]) are distinct; each owner holds at most 2 blocks, and some owner holds exactly 2; owners 0 and 63 each hold at least one block. `slot_table`: paired with owner_table as stated there.
All inputs are finite; a program needn't handle non-finite values.
Results may differ from a plain program's by a relative error of at most 0.0064.
Values may be sent and summed in bfloat16 or wider, within the bound.
A program may use at most 64 MiB of HBM per device.

v0:
```python
import jax
import jax.numpy as jnp
from jax import lax
from jax.sharding import PartitionSpec as P


def per_device(
    gradient, second_moment, owner_table, slot_table, left_stat, right_stat, left_root, right_root
):
    blocks, shard_rows, shard_cols = gradient.shape
    owner_count = lax.axis_size("dp")
    slot_count = left_stat.shape[1]
    stripe = left_stat.shape[2]
    block_order = left_stat.shape[3]
    owner_index = lax.axis_index("dp")
    tensor_index = lax.axis_index("tensor")
    flat_index = owner_table * slot_count + slot_table
    new_second = 0.99 * second_moment + 0.01 * gradient * gradient
    adam = gradient / (jnp.sqrt(new_second) + 1e-08)
    adam_part = jnp.sum(adam * adam, axis=(1, 2))
    grad_low = gradient.astype(jnp.bfloat16)
    gathered = lax.all_gather(grad_low, "tensor", axis=2, tiled=True)
    buffer = (
        jnp.zeros((owner_count * slot_count, shard_rows, block_order), jnp.bfloat16)
        .at[flat_index]
        .set(gathered)
    )
    whole = lax.all_to_all(buffer, "dp", split_axis=0, concat_axis=1, tiled=True)
    row_part = lax.dynamic_slice_in_dim(whole, tensor_index * stripe, stripe, 1)
    col_part = lax.dynamic_slice_in_dim(whole, tensor_index * stripe, stripe, 2)
    left_term = jnp.einsum("sik,sjk->sij", row_part, whole, preferred_element_type=jnp.float32)
    right_term = jnp.einsum("ski,skj->sij", col_part, whole, preferred_element_type=jnp.float32)
    left_new = 0.5 * left_stat + 0.5 / block_order * left_term[None]
    right_new = 0.5 * right_stat + 0.5 / block_order * right_term[None]
    mixed = jnp.einsum(
        "sik,skj->sij", left_root[0], whole, preferred_element_type=jnp.float32
    ).astype(jnp.bfloat16)
    product = jnp.einsum(
        "sik,skj->sij",
        mixed,
        lax.all_gather(right_root[0], "tensor", axis=1, tiled=True),
        preferred_element_type=jnp.float32,
    )
    precond = product.astype(jnp.bfloat16)
    precond_wide = precond.astype(jnp.float32)
    root_slot = jnp.sum(precond_wide * precond_wide, axis=(1, 2))
    returned = lax.all_to_all(
        lax.all_to_all(precond, "tensor", split_axis=2, concat_axis=1, tiled=True),
        "dp",
        split_axis=1,
        concat_axis=0,
        tiled=True,
    )
    returned_blocks = returned[flat_index]
    slot_match = slot_table[:, None] == jnp.arange(slot_count, dtype=jnp.int32)[None, :]
    looked_up = jnp.sum(jnp.where(slot_match, root_slot[None, :], 0.0), axis=1)
    root_part = jnp.where(owner_table == owner_index, looked_up, 0.0)
    adam_total, root_total = lax.psum((adam_part, root_part), ("dp", "tensor"))
    graft_scale = jnp.sqrt(adam_total / (root_total + 1e-06))
    update = (graft_scale[:, None, None] * returned_blocks.astype(jnp.float32)).astype(jnp.bfloat16)
    return (update, new_second, left_new, right_new)


def solution(mesh):
    placed = (
        P(None, "dp", "tensor"),
        P(None, "dp", "tensor"),
        P(),
        P(),
        P("dp", None, "tensor", None),
        P("dp", None, "tensor", None),
        P("dp", None, "tensor", None),
        P("dp", None, "tensor", None),
    )
    return jax.shard_map(
        per_device,
        mesh=mesh,
        in_specs=placed,
        out_specs=(
            P(None, "dp", "tensor"),
            P(None, "dp", "tensor"),
            P("dp", None, "tensor", None),
            P("dp", None, "tensor", None),
        ),
        check_vma=False,
    )
```

profile of v0, /device:TPU:1, one launch (start us, length us, event | category | flops | bytes accessed | tf_op | source)
XLA Modules:
  0.0 296.9 jit_solution(7836436570167904347)
XLA Ops:
  7.2 0.0 copy-start
  7.2 0.0 copy-start.4
  7.2 0.0 copy-start.5
  7.2 0.0 all-gather.4.cloned.1.call-start
  7.2 3.2 %multiply_reduce_fusion.1 = (f32[48]{0:T(128)S(1)}, f32[48,16,256]{2,1,0:T(8,128)}, bf16[48,16,256]{2,1,0:T(8,128)(2,1)}) fusion(f32[48,16,256]{2,1,0:T(8,128)} %param.8, f32[48,16,256]{2,1,0:T(8,128)} %param.9), kind=kLoop, calls=%fused_computation.15 | loop fusion | flops 1769424 | bytes 2752704 | tf_op jit(solution)/shard_map/reduce_sum | solution.py:20
  10.4 0.0 all-gather.4.cloned.1.call-update
  10.5 0.0 copy-done.4
  10.5 0.0 copy-done.5
  10.5 34.7 %all-gather.4.cloned.1.call-done = bf16[48,16,1024]{2,1,0:T(8,128)(2,1)} async-done(((bf16[48,16,256]{2,1,0:T(8,128)(2,1)}), bf16[48,16,1024]{2,1,0:T(8,128)(2,1)}) %all-gather.4.cloned.1.call-update) | async-done | bytes 1572880 | tf_op jit(solution)/shard_map/all_gather | solution.py:22
  45.2 0.0 copy-start.3
  45.2 2.5 broadcast_in_dim.29
  47.7 0.0 copy-done.3
  47.7 6.6 %scatter_fusion = bf16[128,16,1024]{2,1,0:T(8,128)(2,1)} fusion(bf16[128,16,1024]{2,1,0:T(8,128)(2,1)} %broadcast_in_dim.29, s32[48]{0:T(128)S(1)} %compare_select_fusion, bf16[48,16,1024]{2,1,0:T(8,128)(2,1)S(1)} %copy-done.3), kind=kCustom, calls=%fused_computation.1 | custom fusion | bytes 4718784 | tf_op jit(solution)/shard_map/scatter | solution.py:26
  54.3 12.2 %all-to-all-start = ((bf16[128,16,1024]{2,1,0:T(8,128)(2,1)}), bf16[128,16,1024]{2,1,0:T(8,128)(2,1)}, u32[]{:S(2)}, u32[]{:S(2)}) async-start(bf16[128,16,1024]{2,1,0:T(8,128)(2,1)} %scatter_fusion), calls=%async_computation | async-start | bytes 8388608 | tf_op jit(solution)/shard_map/all_to_all | solution.py:28
  66.5 0.0 all-gather.6.cloned.1.call-start
  66.6 0.7 all-gather.6.cloned.1.call-update
  67.3 94.0 %all-to-all-done = bf16[128,16,1024]{2,1,0:T(8,128)(2,1)} async-done(((bf16[128,16,1024]{2,1,0:T(8,128)(2,1)}), bf16[128,16,1024]{2,1,0:T(8,128)(2,1)}, u32[]{:S(2)}, u32[]{:S(2)}) %all-to-all-start) | async-done | bytes 4194336 | tf_op jit(solution)/shard_map/all_to_all | solution.py:28
  161.3 5.0 %copy.34 = bf16[2,64,16,1024]{3,2,1,0:T(8,128)(2,1)} copy(bf16[2,64,16,1024]{3,2,0,1:T(8,128)(2,1)} %bitcast.1) | data formatting | bytes 8388608 | tf_op jit(solution)/shard_map/all_to_all | solution.py:28
  166.2 0.0 all-gather.6.cloned.1.call-done
  166.2 0.0 copy-done
  166.2 6.1 %multiply_reduce_fusion = (f32[2]{0:T(128)S(1)}, bf16[2,256,1024]{2,1,0:T(8,128)(2,1)S(1)}) fusion(bf16[1,2,1024,1024]{3,2,1,0:T(8,128)(2,1)} %all-gather.6.cloned.1.call-done, bf16[2,1024,1024]{2,1,0:T(8,128)(2,1)} %bitcast.33, bf16[1,2,256,1024]{3,2,1,0:T(8,128)(2,1)S(1)} %copy-done), kind=kOutput, calls=%fused_computation.6 | convolution fusion | flops 2150105088 | bytes 10485768 | tf_op jit(solution)/shard_map/sik,skj->sij/dot_general | solution.py:38
  172.4 0.9 copy.37
  173.3 16.3 %all_to_all.54 = bf16[2,256,1024]{1,0,2:T(2,128)(2,1)S(1)} all-to-all(bf16[2,256,1024]{1,0,2:T(2,128)(2,1)S(1)} %copy.37), channel_id=1, replica_groups=mesh['dp'=64,'tensor'=4] {'tensor'}, dimensions={2} | all-to-all | bytes 2097152 | tf_op jit(solution)/shard_map/all_to_all | solution.py:48
  189.6 0.1 copy.38
  189.8 0.5 copy.39
  190.3 2.1 copy.40
  192.4 9.4 %all-to-all-start.2 = ((bf16[2,1024,256]{2,0,1:T(2,128)(2,1)}), bf16[2,1024,256]{2,0,1:T(2,128)(2,1)S(1)}, u32[]{:S(2)}, u32[]{:S(2)}) async-start(bf16[2,1024,256]{2,0,1:T(2,128)(2,1)} %copy.40), calls=%async_computation.2 | async-start | bytes 2097152 | tf_op jit(solution)/shard_map/all_to_all | solution.py:47
  201.8 0.1 fusion.11
  201.9 77.7 %all-reduce = (f32[48]{0:T(128)S(1)}, f32[48]{0:T(128)S(1)}) all-reduce(f32[48]{0:T(128)S(1)} %get-tuple-element.6, f32[48]{0:T(128)S(1)} %compare_select_fusion.2), channel_id=1, replica_groups=mesh['dp'=64,'tensor'=4] {'dp','tensor'}, use_global_device_ids=true, to_apply=%region_1.0 | all-reduce | flops 96 | bytes 768 | tf_op jit(solution)/shard_map/psum | solution.py:58
  279.6 0.0 copy-start.1
  279.6 0.0 copy-start.2
  279.6 6.0 %bitcast_add_fusion = f32[1,2,256,1024]{3,2,1,0:T(8,128)} fusion(f32[1,2,256,1024]{3,2,1,0:T(8,128)} %param.13, bf16[2,1024,1024]{2,1,0:T(8,128)(2,1)} %bitcast.34, s32[]{:T(128)S(6)} %select_n.19), kind=kOutput, calls=%fused_computation.4 | convolution fusion | flops 1075314688 | bytes 9437188 | tf_op jit(solution)/shard_map/ski,skj->sij/dot_general | solution.py:32
  285.6 0.0 copy-done.1
  285.6 0.0 copy-done.2
  285.6 2.7 bitcast_add_fusion.1
  288.3 0.0 all-to-all-done.2
  288.3 0.1 copy.41
  288.4 0.1 copy.42
  288.5 0.6 gather_fusion
  289.1 0.9 multiply_convert_fusion
  (4 shorter events, 0.0 us)
Async XLA Ops:
  7.2 159.1 %copy-start = (bf16[1,2,256,1024]{3,2,1,0:T(8,128)(2,1)S(1)}, bf16[1,2,256,1024]{3,2,1,0:T(8,128)(2,1)}, u32[]{:S(2)}) copy-start(bf16[1,2,256,1024]{3,2,1,0:T(8,128)(2,1)} %param.14) | copy-start | bytes 3145732
  7.2 3.3 %copy-start.4 = (s32[48]{0:T(128)S(1)}, s32[48]{0:T(128)}, u32[]{:S(2)}) copy-start(s32[48]{0:T(128)} %param.10) | copy-start | bytes 580
  7.2 3.3 %copy-start.5 = (s32[48]{0:T(128)S(1)}, s32[48]{0:T(128)}, u32[]{:S(2)}) copy-start(s32[48]{0:T(128)} %param.11) | copy-start | bytes 580
  7.2 38.0 %all-gather.4.cloned.1.call-start = ((), (), s32[]{:S(2)}) async-start(), calls=%async_computation.3 | async-start | bytes 1966080 | tf_op jit(solution)/shard_map/all_gather | solution.py:22
  45.2 2.5 copy-start.3
  54.3 107.0 %all-to-all-start = ((bf16[128,16,1024]{2,1,0:T(8,128)(2,1)}), bf16[128,16,1024]{2,1,0:T(8,128)(2,1)}, u32[]{:S(2)}, u32[]{:S(2)}) async-start(bf16[128,16,1024]{2,1,0:T(8,128)(2,1)} %scatter_fusion), calls=%async_computation | async-start | bytes 8388608 | tf_op jit(solution)/shard_map/all_to_all | solution.py:28
  66.5 99.7 %all-gather.6.cloned.1.call-start = ((), (), s32[]{:S(2)}) async-start(), calls=%async_computation.4 | async-start | bytes 5242880 | tf_op jit(solution)/shard_map/all_gather | solution.py:41
  192.4 95.9 %all-to-all-start.2 = ((bf16[2,1024,256]{2,0,1:T(2,128)(2,1)}), bf16[2,1024,256]{2,0,1:T(2,128)(2,1)S(1)}, u32[]{:S(2)}, u32[]{:S(2)}) async-start(bf16[2,1024,256]{2,0,1:T(2,128)(2,1)} %copy.40), calls=%async_computation.2 | async-start | bytes 2097152 | tf_op jit(solution)/shard_map/all_to_all | solution.py:47
  279.6 6.0 %copy-start.1 = (bf16[2,64,16,1024]{3,2,1,0:T(8,128)(2,1)S(1)}, bf16[2,64,16,1024]{3,2,1,0:T(8,128)(2,1)}, u32[]{:S(2)}) copy-start(bf16[2,64,16,1024]{3,2,1,0:T(8,128)(2,1)} %copy.34) | copy-start | bytes 12582916
  279.6 6.0 %copy-start.2 = (f32[1,2,256,1024]{3,2,1,0:T(8,128)S(1)}, f32[1,2,256,1024]{3,2,1,0:T(8,128)}, u32[]{:S(2)}) copy-start(f32[1,2,256,1024]{3,2,1,0:T(8,128)} %param.12) | copy-start | bytes 6291460
Sparse Core Ops, SparseCore 0:
  10.6 34.5 all-gather.3
  69.2 51.1 all-gather.5
where the time goes:
time: 298 us; the launch traced here: 297 us
  waiting for transfers between devices  129 us (43%)
  blocking collectives  94 us (32%)
  starting transfers between devices  21.8 us (7%)
  local copies, waits for them, and re-layouts  18.6 us (6%)
  matrix products  14.8 us (5%)
  between operations  14.2 us (5%)
  other arithmetic  4.19 us (1%)
    all_to_all x1, waiting for transfers between devices, per_device(): lax.all_to_all(buffer, 'dp', split_axis=0, concat_axis=1, tiled=True)  94 us
    psum x1, blocking collectives, per_device(): adam_total, root_total = lax.psum((adam_part, root_part), ('dp', 'tensor'))  77.7 us
    all_gather x1, waiting for transfers between devices, per_device(): gathered = lax.all_gather(grad_low, 'tensor', axis=2, tiled=True)  34.7 us
    all_to_all x1, blocking collectives, per_device(): lax.all_to_all(precond, 'tensor', split_axis=2, concat_axis=1, tiled=True)  16.3 us
    all_to_all x1, starting transfers between devices, per_device(): lax.all_to_all(buffer, 'dp', split_axis=0, concat_axis=1, tiled=True)  12.2 us
    all_to_all x1, starting transfers between devices, per_device(): lax.all_to_all(lax.all_to_all(precond, 'tensor', split_axis=2, concat_axi...  9.43 us
    scatter x1, local copies, waits for them, and re-layouts, per_device(): buffer = jnp.zeros((owner_count * slot_count, shard_rows, block_order), j...  6.61 us
    dot_general x1, matrix products, per_device(): jnp.einsum('sik,skj->sij', mixed, lax.all_gather(right_root[0], 'tensor',...  6.14 us
  transfers between devices with their start and end apart: 4, of which 2 were waited for; matrix products, arithmetic and copies ran while one was open for 5% of the time, Pallas kernels for 0%

commit v1 on v0

v1 whole, which is shorter than its diff:
```python
import functools

import jax
import jax.numpy as jnp
from jax import lax
from jax.experimental import pallas as pl
from jax.experimental.pallas import tpu as pltpu
from jax.sharding import PartitionSpec as P

MESH = pl.DeviceIdType.MESH
NX, NY, NZ, NC = 4, 4, 8, 2


def position():
    dp = lax.axis_index("dp")
    x = lax.axis_index("tensor")
    return x, (dp // NC) % NY, dp // (NC * NY), dp % NC


def device(x, y, z, c):
    return ((z * NY + y) * NC + c, x)


def entry_barrier(x, y, z, c):
    barrier = pltpu.get_barrier_semaphore()
    partners = [(x, y, (z + k) % NZ, c) for k in range(1, NZ)]
    partners += [(x, (y + k) % NY, z, c) for k in range(1, NY)]
    partners += [((x + k) % NX, y, z, h) for k in range(1, NX) for h in range(NC)]
    partners += [(x, y, z, 1 - c)]
    for partner in partners:
        pl.semaphore_signal(barrier, inc=1, device_id=device(*partner), device_id_type=MESH)
    pl.semaphore_wait(barrier, len(partners))


def remote(src, dst, send_sem, recv_sem, target):
    return pltpu.make_async_remote_copy(
        src_ref=src,
        dst_ref=dst,
        send_sem=send_sem,
        recv_sem=recv_sem,
        device_id=device(*target),
        device_id_type=MESH,
    )


def either(is_self, src, dst, send_sem, recv_sem, target):
    @pl.when(is_self)
    def _():
        pltpu.make_async_copy(src, dst, recv_sem).start()

    @pl.when(jnp.logical_not(is_self))
    def _():
        remote(src, dst, send_sem, recv_sem, target).start()


Z_ORDER = (4, 3, 5, 2, 6, 1, 7)
Y_ORDER = (2, 1, 3)
IN_ORDER = (2, 1, 3, 0)
OUT_ORDER = (0, 1, 3, 2)


def gather_kernel(
    slots, lroot, rroot, whole, left, right, zr, yr,
    z_send, z_recv, y_send, y_recv, x_send, x_recv, c_send, c_recv,
    l_send, l_recv, r_send, r_recv, f_send, f_recv,
):
    x, y, z, c = position()
    entry_barrier(x, y, z, c)
    width = slots.shape[4]

    def z_copy(j, k):
        to = (z + k) % NZ
        return remote(
            slots.at[to, :, (x + j) % NX], zr.at[j, :, z],
            z_send.at[j, k], z_recv.at[j, k], (x, y, to, c),
        )

    def z_own(j):
        return pltpu.make_async_copy(slots.at[z, :, (x + j) % NX], zr.at[j, :, z], z_recv.at[j, 0])

    def y_copy(j, k):
        to = (y + k) % NY
        return remote(
            zr.at[j, to], yr.at[j, :, y], y_send.at[j, k], y_recv.at[j, k], (x, to, z, c)
        )

    def y_own(j):
        return pltpu.make_async_copy(zr.at[j, y], yr.at[j, :, y], y_recv.at[j, 0])

    def cols(index):
        return pl.ds(pl.multiple_of(index * width, width), width)

    def x_copy(j):
        to = (x + j) % NX
        return remote(
            yr.at[j], whole.at[:, :, c, :, cols(x)],
            x_send.at[j], x_recv.at[j], (to, y, z, c),
        )

    def x_own():
        return pltpu.make_async_copy(yr.at[0], whole.at[:, :, c, :, cols(x)], x_recv.at[0])

    def c_copy(j):
        part = whole.at[:, :, c, :, cols((x - j + NX) % NX)]
        return remote(part, part, c_send.at[j], c_recv.at[j], (x, y, z, 1 - c))

    def root_args(s, h):
        to = NC * c + s
        is_self = jnp.logical_and(to == x, c == h)
        return is_self, to

    def forward(i):
        part = right.at[i, c]
        return remote(part, part, f_send.at[i], f_recv.at[i], (x, y, z, 1 - c))

    for k in Z_ORDER:
        z_copy(IN_ORDER[0], k).start()
    z_own(IN_ORDER[0]).start()
    for s in range(2):
        for h in range(NC):
            is_self, to = root_args(s, h)
            either(is_self, lroot.at[s, :, h], left.at[x], l_send.at[s, h], l_recv.at[x], (to, y, z, h))
    for s in range(2):
        for h in range(NC):
            is_self, to = root_args(s, h)
            either(is_self, rroot.at[s, h], right.at[x, h], r_send.at[s, h], r_recv.at[x], (to, y, z, h))
    for j in IN_ORDER[1:]:
        for k in Z_ORDER:
            z_copy(j, k).start()
        z_own(j).start()

    def finish_y(j):
        for k in Y_ORDER:
            y_copy(j, k).wait_recv()
        y_own(j).wait()
        if j == 0:
            x_own().start()
        else:
            x_copy(j).start()

    def finish_x(j):
        if j == 0:
            x_own().wait()
        else:
            x_copy(j).wait_recv()
        c_copy(j).start()

    for i, j in enumerate(IN_ORDER):
        for k in Z_ORDER:
            z_copy(j, k).wait_recv()
        z_own(j).wait()
        for k in Y_ORDER:
            y_copy(j, k).start()
        y_own(j).start()
        if i >= 1:
            finish_y(IN_ORDER[i - 1])
    finish_y(IN_ORDER[-1])
    for i in range(NX):
        pltpu.make_async_copy(right.at[i, c], right.at[i, c], r_recv.at[i]).wait()
        forward(i).start()
    for j in IN_ORDER:
        finish_x(j)
    for i in range(NX):
        pltpu.make_async_copy(left.at[i], left.at[i], l_recv.at[i]).wait()
        forward(i).wait()
    for j in IN_ORDER:
        c_copy(j).wait()
        if j != 0:
            x_copy(j).wait_send()
        for k in Y_ORDER:
            y_copy(j, k).wait_send()
        for k in Z_ORDER:
            z_copy(j, k).wait_send()
    for s in range(2):
        for h in range(NC):
            is_self, to = root_args(s, h)

            @pl.when(jnp.logical_not(is_self))
            def _():
                remote(lroot.at[s, :, h], left.at[x], l_send.at[s, h], l_recv.at[x], (to, y, z, h)).wait_send()
                remote(rroot.at[s, h], right.at[x, h], r_send.at[s, h], r_recv.at[x], (to, y, z, h)).wait_send()


def scatter_kernel(
    precond, lterm, rterm, row, back, left, right, rows, xr, yr,
    z_send, z_recv, y_send, y_recv, x_send, x_recv,
    l_send, l_recv, r_send, r_recv, n_send, n_recv,
):
    x, y, z, c = position()
    entry_barrier(x, y, z, c)
    width = back.shape[4]

    def cols(index):
        return pl.ds(pl.multiple_of(index * width, width), width)

    def x_copy(j):
        to = (x + j) % NX
        return remote(
            precond.at[:, :, :, cols(to)], xr.at[j], x_send.at[j], x_recv.at[j], (to, y, z, c)
        )

    def x_own():
        return pltpu.make_async_copy(precond.at[:, :, :, cols(x)], xr.at[0], x_recv.at[0])

    def y_copy(j, k):
        to = (y + k) % NY
        return remote(
            xr.at[j, :, to], yr.at[j, :, y], y_send.at[j, k], y_recv.at[j, k], (x, to, z, c)
        )

    def y_own(j):
        return pltpu.make_async_copy(xr.at[j, :, y], yr.at[j, :, y], y_recv.at[j, 0])

    def z_copy(j, k):
        to = (z + k) % NZ
        return remote(
            yr.at[j, to], back.at[z, :, (x - j + NX) % NX],
            z_send.at[j, k], z_recv.at[j, k], (x, y, to, c),
        )

    def z_own(j):
        return pltpu.make_async_copy(yr.at[j, z], back.at[z, :, (x - j + NX) % NX], z_recv.at[j, 0])

    def n_copies(stage):
        if stage == 0:
            src = dst = rows.at[c, x, y, z]
            targets = [(x, y, (z + k) % NZ, c) for k in range(1, NZ)]
        elif stage == 1:
            src = dst = rows.at[c, x, y]
            targets = [(x, (y + k) % NY, z, c) for k in range(1, NY)]
        elif stage == 2:
            src = dst = rows.at[c, x]
            targets = [((x + k) % NX, y, z, c) for k in range(1, NX)]
        else:
            src = dst = rows.at[c]
            targets = [(x, y, z, 1 - c)]
        return [
            remote(src, dst, n_send.at[stage, i], n_recv.at[stage, i], target)
            for i, target in enumerate(targets)
        ]

    own_row = pltpu.make_async_copy(row, rows.at[c, x, y, z], n_recv.at[0, NZ - 1])
    own_row.start()
    x_own().start()
    for j in OUT_ORDER[1:]:
        x_copy(j).start()
    owner = x // 2
    slot = x % 2
    for i in range(1, NX + 1):
        to = (x + i) % NX
        is_self = jnp.logical_and(to == x, c == owner)
        either(is_self, lterm.at[to], left.at[slot, :, c], l_send.at[i - 1], l_recv.at[x, c], (to, y, z, owner))
    for i in range(2):
        to = NC * c + i
        is_self = jnp.logical_and(to == x, c == owner)
        either(is_self, rterm.at[i], right.at[slot], r_send.at[i], r_recv.at[slot], (to, y, z, owner))
    own_row.wait()
    for copy in n_copies(0):
        copy.start()

    def finish_y(j):
        for k in Y_ORDER:
            y_copy(j, k).wait_recv()
        y_own(j).wait()
        for k in Z_ORDER:
            z_copy(j, k).start()
        z_own(j).start()

    for i, j in enumerate(OUT_ORDER):
        if j == 0:
            x_own().wait()
        else:
            x_copy(j).wait_recv()
        for k in Y_ORDER:
            y_copy(j, k).start()
        y_own(j).start()
        if i >= 1:
            finish_y(OUT_ORDER[i - 1])
        for copy in n_copies(i):
            copy.wait_recv()
        if i < 3:
            for copy in n_copies(i + 1):
                copy.start()
    finish_y(OUT_ORDER[-1])
    for i in range(2):
        for h in range(NC):
            part = left.at[i, :, h]
            pltpu.make_async_copy(part, part, l_recv.at[NC * c + i, h]).wait()
        part = right.at[i]
        pltpu.make_async_copy(part, part, r_recv.at[i]).wait()
    for j in OUT_ORDER:
        for k in Z_ORDER:
            z_copy(j, k).wait()
        z_own(j).wait()
        for k in Y_ORDER:
            y_copy(j, k).wait_send()
        if j != 0:
            x_copy(j).wait_send()
    for stage in range(4):
        for copy in n_copies(stage):
            copy.wait_send()
    for i in range(1, NX + 1):
        to = (x + i) % NX

        @pl.when(jnp.logical_not(jnp.logical_and(to == x, c == owner)))
        def _():
            remote(lterm.at[to], left.at[slot, :, c], l_send.at[i - 1], l_recv.at[x, c], (to, y, z, owner)).wait_send()

    for i in range(2):
        to = NC * c + i

        @pl.when(jnp.logical_not(jnp.logical_and(to == x, c == owner)))
        def _():
            remote(rterm.at[i], right.at[slot], r_send.at[i], r_recv.at[slot], (to, y, z, owner)).wait_send()


ANY = pl.BlockSpec(memory_space=pl.ANY)
VMEM = pl.BlockSpec(memory_space=pltpu.VMEM)
DMA = pltpu.SemaphoreType.DMA


def per_device(
    gradient, second_moment, owner_table, slot_table, left_stat, right_stat, left_root, right_root
):
    blocks, rows, width = gradient.shape
    order = left_stat.shape[3]
    stripe = left_stat.shape[2]
    low = jnp.bfloat16
    slots = NZ * NY * NC * 2
    x, y, z, c = position()
    flat = owner_table * 2 + slot_table

    new_second = 0.99 * second_moment + 0.01 * gradient * gradient
    adam = gradient / (jnp.sqrt(new_second) + 1e-08)
    adam_part = jnp.sum(adam * adam, axis=(1, 2))
    grad_low = gradient.astype(low)
    match = flat[None, :] == jnp.arange(slots, dtype=jnp.int32)[:, None]
    taken = jnp.any(match, axis=1)
    source = jnp.sum(jnp.where(match, jnp.arange(blocks, dtype=jnp.int32)[None, :], 0), axis=1)
    slot_grad = jnp.where(taken[:, None, None], grad_low[source], jnp.zeros((), low))

    groups = stripe // (NC * rows)
    shape = jax.ShapeDtypeStruct
    whole, lroot, rroot = pl.pallas_call(
        gather_kernel,
        out_shape=(
            shape((NZ, NY, NC, rows, order), low),
            shape((NX, groups, rows, order), low),
            shape((NX, NC, stripe // NC, order), low),
        ),
        in_specs=[VMEM] * 3,
        out_specs=(ANY, ANY, ANY),
        scratch_shapes=[
            pltpu.VMEM((NX, NY, NZ, rows, width), low),
            pltpu.VMEM((NX, NZ, NY, rows, width), low),
            DMA((NX, NZ)), DMA((NX, NZ)), DMA((NX, NY)), DMA((NX, NY)),
            DMA((NX,)), DMA((NX,)), DMA((NX,)), DMA((NX,)),
            DMA((2, NC)), DMA((NX,)), DMA((2, NC)), DMA((NX,)), DMA((NX,)), DMA((NX,)),
        ],
        compiler_params=pltpu.CompilerParams(collective_id=0, has_side_effects=True),
        name="gather_blocks",
    )(
        slot_grad.reshape(NZ, NY, NX, rows, width),
        left_root.reshape(2, groups, NC, rows, order),
        right_root.reshape(2, NC, stripe // NC, order),
    )

    block = whole.reshape(order, order)
    half = order // NC
    own_rows = lax.dynamic_index_in_dim(whole, c, 2, False).reshape(half, order)
    own_cols = lax.dynamic_slice_in_dim(block, c * half, half, 1)
    dot = functools.partial(lax.dot_general, preferred_element_type=jnp.float32)
    mixed = dot(lroot.reshape(half, order), block, (((1,), (0,)), ((), ()))).astype(low)
    precond = dot(mixed, rroot.reshape(order, order), (((1,), (0,)), ((), ()))).astype(low)
    wide = precond.astype(jnp.float32)
    root_part = jnp.sum(wide * wide)
    factor = 0.5 / order
    lterm = (factor * dot(own_rows, block, (((1,), (1,)), ((), ())))).astype(low)
    rterm = (factor * dot(own_cols, block, (((0,), (0,)), ((), ())))).astype(low)

    row = jnp.concatenate(
        [adam_part, jnp.full((1,), root_part), jnp.zeros((128 - blocks - 1,), jnp.float32)]
    ).reshape(1, 128)
    back, left_term, right_term, all_rows = pl.pallas_call(
        scatter_kernel,
        out_shape=(
            shape((NZ, NY, NX, rows, width), low),
            shape((2, groups, NC, rows, order), low),
            shape((2, stripe, order), low),
            shape((NC, NX, NY, NZ, 1, 128), jnp.float32),
        ),
        in_specs=[VMEM] * 4,
        out_specs=(ANY,) * 4,
        scratch_shapes=[
            pltpu.VMEM((NX, NZ, NY, rows, width), low),
            pltpu.VMEM((NX, NZ, NY, rows, width), low),
            DMA((NX, NZ)), DMA((NX, NZ)), DMA((NX, NY)), DMA((NX, NY)),
            DMA((NX,)), DMA((NX,)),
            DMA((NX,)), DMA((NX, NC)), DMA((2,)), DMA((2,)),
            DMA((4, NZ)), DMA((4, NZ)),
        ],
        compiler_params=pltpu.CompilerParams(collective_id=1, has_side_effects=True),
        name="scatter_blocks",
    )(
        precond.reshape(NZ, NY, rows, order),
        lterm.reshape(NX, groups, rows, order),
        rterm.reshape(2, stripe, order),
        row,
    )

    left_new = 0.5 * left_stat + left_term.reshape(left_stat.shape).astype(jnp.float32)
    right_new = 0.5 * right_stat + right_term.reshape(right_stat.shape).astype(jnp.float32)
    adam_total = jnp.sum(all_rows[..., :blocks], axis=(0, 1, 2, 3, 4))
    root_slot = jnp.sum(all_rows[..., 0, blocks], axis=0).transpose(2, 1, 0).reshape(1, slots)
    root_total = jnp.sum(jnp.where(match.T, root_slot, 0.0), axis=1)
    scale = jnp.sqrt(adam_total / (root_total + 1e-06))
    returned = back.reshape(slots, rows, width)[flat]
    update = (scale[:, None, None] * returned.astype(jnp.float32)).astype(low)
    return (update, new_second, left_new, right_new)


def solution(mesh):
    placed = (
        P(None, "dp", "tensor"),
        P(None, "dp", "tensor"),
        P(),
        P(),
        P("dp", None, "tensor", None),
        P("dp", None, "tensor", None),
        P("dp", None, "tensor", None),
        P("dp", None, "tensor", None),
    )
    return jax.shard_map(
        per_device,
        mesh=mesh,
        in_specs=placed,
        out_specs=(
            P(None, "dp", "tensor"),
            P(None, "dp", "tensor"),
            P("dp", None, "tensor", None),
            P("dp", None, "tensor", None),
        ),
        check_vma=False,
    )
```

time: 298 us -> 142 us (0.48)
  waiting for transfers between devices: 129 us -> 0 us
  Pallas kernels: 0 us -> 107 us
  blocking collectives: 94 us -> 0 us
  starting transfers between devices: 21.8 us -> 0 us
  local copies, waits for them, and re-layouts: 18.6 us -> 4.58 us
  between operations: 14.2 us -> 0.74 us
  other arithmetic: 4.19 us -> 17.3 us
  matrix products: 14.8 us -> 11.1 us
    pallas_call x0 -> x2, Pallas kernels: none -> 107 us  [the longest x1 55.2 us: per_device(): pl.pallas_call(scatter_kernel, out_shape=(shape((NZ, NY, NX, rows, width)...]
    all_to_all x2 -> x0, waiting for transfers between devices: 94 us -> none  [the longest x1 94 us: per_device(): lax.all_to_all(buffer, 'dp', split_axis=0, concat_axis=1, tiled=True)]
    psum x1 -> x0, blocking collectives: 77.7 us -> none  [per_device(): adam_total, root_total = lax.psum((adam_part, root_part), ('dp', 'tensor'))]
    all_gather x2 -> x0, waiting for transfers between devices: 34.7 us -> none  [the longest x1 34.7 us: per_device(): gathered = lax.all_gather(grad_low, 'tensor', axis=2, tiled=True)]
    all_to_all x2 -> x0, starting transfers between devices: 21.7 us -> none  [the longest x1 12.2 us: per_device(): lax.all_to_all(buffer, 'dp', split_axis=0, concat_axis=1, tiled=True)]
    all_to_all x1 -> x0, blocking collectives: 16.3 us -> none  [per_device(): lax.all_to_all(precond, 'tensor', split_axis=2, concat_axis=1, tiled=True)]
    all_to_all x6 -> x0, local copies, waits for them, and re-layouts: 7.95 us -> none  [the longest x1 4.98 us: per_device(): lax.all_to_all(buffer, 'dp', split_axis=0, concat_axis=1, tiled=True)]
    scatter x1 -> x0, local copies, waits for them, and re-layouts: 6.61 us -> none  [per_device(): buffer = jnp.zeros((owner_count * slot_count, shard_rows, block_order), j...]
  transfers between devices with their start and end apart: 4 -> 0, of which waited for: 2 -> 0; matrix products, arithmetic and copies ran while one was open for 5% -> 0% of each run, Pallas kernels for 0% -> 0%
where the time goes in v1:
time: 142 us; the launch traced here: 141 us
  Pallas kernels  107 us (75%)
  other arithmetic  17.3 us (12%)
  matrix products  11.1 us (8%)
  local copies, waits for them, and re-layouts  4.58 us (3%)
    pallas_call x1, Pallas kernels, per_device(): pl.pallas_call(scatter_kernel, out_shape=(shape((NZ, NY, NX, rows, width)...  55.2 us
    pallas_call x1, Pallas kernels, per_device(): pl.pallas_call(gather_kernel, out_shape=(shape((NZ, NY, NC, rows, order),...  52 us
    dot_general x1, matrix products, per_device(): dot(mixed, rroot.reshape(order, order), (((1,), (0,)), ((), ())))  6.6 us
    add x1, other arithmetic, per_device(): 0.5 * right_stat + right_term.reshape(right_stat.shape).astype(jnp.float32)  4.76 us
    reduce_sum x1, other arithmetic, per_device(): adam_part = jnp.sum(adam * adam, axis=(1, 2))  3 us

profile of v1, /device:TPU:1, one launch (start us, length us, event | category | flops | bytes accessed | tf_op | source)
XLA Modules:
  0.0 140.9 jit_solution(7396379807375246249)
XLA Ops:
  0.7 0.7 compare_select_fusion
  1.3 0.0 copy-start.3
  1.3 0.1 select_reduce_fusion.1
  1.4 0.4 copy-done.3
  1.9 0.1 fusion.2
  2.0 0.1 broadcast_in_dim.55
  2.1 3.0 %multiply_reduce_fusion.1 = (f32[48]{0:T(128)S(1)}, f32[48,16,256]{2,1,0:T(8,128)}, bf16[48,16,256]{2,1,0:T(8,128)(2,1)S(1)}) fusion(f32[48,16,256]{2,1,0:T(8,128)} %param.8, f32[48,16,256]{2,1,0:T(8,128)} %param.9), kind=kLoop, calls=%fused_computation.14 | loop fusion | flops 1769424 | bytes 2752704 | tf_op jit(solution)/shard_map/reduce_sum | solution.py:335
  5.1 0.6 gather_fusion
  5.8 1.2 broadcast_select_fusion.slots
  6.9 52.0 %gather_blocks.1 = (bf16[8,4,2,16,1024]{4,3,2,1,0:T(8,128)(2,1)}, bf16[4,8,16,1024]{3,2,1,0:T(8,128)(2,1)}, bf16[4,2,128,1024]{3,2,1,0:T(8,128)(2,1)}) custom-call(bf16[8,4,4,16,256]{4,3,2,1,0:T(8,128)(2,1)} %broadcast_select_fusion.slots, bf16[2,8,2,16,1024]{4,3,2,1,0:T(8,128)(2,1)} %bitcast.31, bf16[2,2,128,1024]{3,2,1,0:T(8,128)(2,1)} %bitcast.32), custom_call_target="tpu_custom_call" | custom-call | tf_op jit(solution)/shard_map/gather_blocks/pallas_call | solution.py:344
  59.0 0.0 copy-start.2
  59.0 6.6 %multiply_reduce_fusion = (f32[]{:T(128)}, bf16[512,1024]{1,0:T(8,128)(2,1)}) fusion(bf16[1024,1024]{1,0:T(8,128)(2,1)} %bitcast.43, bf16[512,1024]{1,0:T(8,128)(2,1)} %bitcast.44, bf16[1024,1024]{1,0:T(8,128)(2,1)} %bitcast.38), kind=kOutput, calls=%fused_computation.4 | convolution fusion | flops 2150105088 | bytes 6291460 | tf_op jit(solution)/shard_map/dot_general | solution.py:374
  65.6 1.3 maximum_bitcast_fusion.row
  66.8 0.0 copy-done.2
  66.8 2.3 %multiply_convert_fusion = bf16[512,1024]{1,0:T(8,128)(2,1)} fusion(bf16[1024,1024]{1,0:T(8,128)(2,1)S(1)} %bitcast.39, s32[]{:T(128)S(6)} %select_n.45), kind=kOutput, calls=%fused_computation.5 | convolution fusion | flops 1074790400 | bytes 4194308 | tf_op jit(solution)/shard_map/dot_general | solution.py:379
  69.1 0.1 constant_dynamic-slice_fusion
  69.2 2.3 %multiply_convert_fusion.1 = bf16[512,1024]{1,0:T(8,128)(2,1)} fusion(bf16[512,1024]{1,0:T(8,128)(2,1)S(1)} %bitcast.34, bf16[1024,1024]{1,0:T(8,128)(2,1)S(1)} %bitcast.40), kind=kOutput, calls=%fused_computation.6 | convolution fusion | flops 1074790400 | bytes 4194304 | tf_op jit(solution)/shard_map/dot_general | solution.py:378
  71.5 0.0 copy-start
  71.5 55.2 %scatter_blocks.1 = (bf16[8,4,4,16,256]{4,3,2,1,0:T(8,128)(2,1)}, bf16[2,8,2,16,1024]{4,3,2,1,0:T(8,128)(2,1)}, bf16[2,256,1024]{2,1,0:T(8,128)(2,1)}, f32[2,4,4,8,1,128]{5,4,3,2,1,0:T(1,128)}) custom-call(bf16[8,4,16,1024]{3,2,1,0:T(8,128)(2,1)} %bitcast.35, bf16[4,8,16,1024]{3,2,1,0:T(8,128)(2,1)} %bitcast.37, bf16[2,256,1024]{2,1,0:T(8,128)(2,1)} %bitcast.36, ...), custom_call_target="tpu_custom_call" | custom-call | tf_op jit(solution)/shard_map/scatter_blocks/pallas_call | solution.py:384
  126.6 0.0 copy-start.1
  126.6 1.9 %gather_fusion.1 = bf16[48,16,256]{2,1,0:T(8,128)(2,1)S(1)} fusion(bf16[128,16,256]{2,1,0:T(8,128)(2,1)} %bitcast.41, s32[1024]{0:T(1024)S(1)} %pad_clamp_fusion), kind=kCustom, calls=%fused_computation.1 | custom fusion | bytes 786624 | tf_op jit(solution)/shard_map/gather | solution.py:417
  128.5 1.7 %slice_reduce_fusion.1 = f32[48]{0:T(128)} fusion(f32[2,4,4,8,1,128]{5,4,3,2,1,0:T(1,128)} %get-tuple-element.14), kind=kLoop, calls=%fused_computation.16 | loop fusion | flops 12240 | bytes 49344 | tf_op jit(solution)/shard_map/reduce_sum | solution.py:413
  130.2 2.1 %slice_reduce_fusion = f32[4,4,8]{2,1,0:T(4,128)} fusion(f32[2,4,4,8,1,128]{5,4,3,2,1,0:T(1,128)} %get-tuple-element.14), kind=kLoop, calls=%fused_computation.15 | loop fusion | flops 128 | bytes 1536 | tf_op jit(solution)/shard_map/reduce_sum | solution.py:414
  132.3 0.8 copy.13
  133.1 0.6 broadcast_in_dim.62
  133.7 0.8 select_reduce_fusion
  134.6 0.7 fusion.5
  135.3 0.9 multiply_convert_fusion.2
  136.1 0.0 copy-done
  136.2 0.0 copy-done.1
  136.2 4.8 %convert_add_fusion = (f32[1,2,256,1024]{3,2,1,0:T(8,128)}, f32[1,2,256,1024]{3,2,1,0:T(8,128)}) fusion(f32[1,2,256,1024]{3,2,1,0:T(8,128)S(1)} %copy-done, bf16[2,256,1024]{2,1,0:T(8,128)(2,1)} %get-tuple-element.17, bf16[1,2,256,1024]{3,2,1,0:T(8,128)(2,1)S(1)} %bitcast.33, f32[1,2,256,1024]{3,2,1,0:T(8,128)} %param.12), kind=kLoop, calls=%fused_computation.2 | loop fusion | flops 3145728 | bytes 10485760 | tf_op jit(solution)/shard_map/add | solution.py:412
  (4 shorter events, 0.0 us)
Async XLA Ops:
  1.3 0.5 copy-start.3
  59.0 7.9 %copy-start.2 = (bf16[8,4,2,16,1024]{4,3,2,1,0:T(8,128)(2,1)S(1)}, bf16[8,4,2,16,1024]{4,3,2,1,0:T(8,128)(2,1)}, u32[]{:S(2)}) copy-start(bf16[8,4,2,16,1024]{4,3,2,1,0:T(8,128)(2,1)} %get-tuple-element.12) | copy-start | bytes 6291460
  71.5 64.7 %copy-start = (f32[1,2,256,1024]{3,2,1,0:T(8,128)S(1)}, f32[1,2,256,1024]{3,2,1,0:T(8,128)}, u32[]{:S(2)}) copy-start(f32[1,2,256,1024]{3,2,1,0:T(8,128)} %param.13) | copy-start | bytes 6291460
  126.6 9.5 %copy-start.1 = (bf16[2,8,2,16,1024]{4,3,2,1,0:T(8,128)(2,1)S(1)}, bf16[2,8,2,16,1024]{4,3,2,1,0:T(8,128)(2,1)}, u32[]{:S(2)}) copy-start(bf16[2,8,2,16,1024]{4,3,2,1,0:T(8,128)(2,1)} %get-tuple-element.16) | copy-start | bytes 3145732

commit v2 on v0

v2 whole, which is shorter than its diff:
```python
import functools

import jax
import jax.numpy as jnp
from jax import lax
from jax.experimental import pallas as pl
from jax.experimental.pallas import tpu as pltpu
from jax.sharding import PartitionSpec as P

MESH = pl.DeviceIdType.MESH
NX, NY, NZ, NC = 4, 4, 8, 2


def position():
    dp = lax.axis_index("dp")
    x = lax.axis_index("tensor")
    return x, (dp // NC) % NY, dp // (NC * NY), dp % NC


def device(x, y, z, c):
    return ((z * NY + y) * NC + c, x)


def entry_barrier(x, y, z, c):
    barrier = pltpu.get_barrier_semaphore()
    partners = [(x, y, (z + k) % NZ, c) for k in range(1, NZ)]
    partners += [(x, (y + k) % NY, z, c) for k in range(1, NY)]
    partners += [((x + k) % NX, y, z, h) for k in range(1, NX) for h in range(NC)]
    partners += [(x, y, z, 1 - c)]
    for partner in partners:
        pl.semaphore_signal(barrier, inc=1, device_id=device(*partner), device_id_type=MESH)
    pl.semaphore_wait(barrier, len(partners))


def remote(src, dst, send_sem, recv_sem, target):
    return pltpu.make_async_remote_copy(
        src_ref=src,
        dst_ref=dst,
        send_sem=send_sem,
        recv_sem=recv_sem,
        device_id=device(*target),
        device_id_type=MESH,
    )


Z_ORDER = (4, 3, 5, 2, 6, 1, 7)
RING = (2, 1, 3)
IN_ORDER = (2, 1, 3, 0)
OUT_ORDER = (0, 1, 3, 2)
LOW = jnp.bfloat16
FULL = jnp.float32


def front_kernel(rank, gradient, second_moment, new_second, send, row):
    step = pl.program_id(0)
    blocks = gradient.shape[0]
    g = gradient[...]
    refreshed = 0.99 * second_moment[...] + 0.01 * g * g
    new_second[...] = refreshed
    adam = g / (jnp.sqrt(refreshed) + 1e-08)
    total = jnp.sum(jnp.sum(adam * adam, axis=1), axis=1, keepdims=True)
    low = g.astype(LOW)
    for b in range(blocks):
        place = rank[step * blocks + b]
        send[place % NX, place // NX] = low[b]
    lane = lax.broadcasted_iota(jnp.int32, (blocks, 128), 1)
    block = lax.broadcasted_iota(jnp.int32, (blocks, 128), 0) + step * blocks
    part = jnp.sum(jnp.where(lane == block, total, 0.0), axis=0, keepdims=True)

    @pl.when(step == 0)
    def _():
        row[...] = jnp.zeros_like(row)

    row[...] += part


def step_kernel(
    table, send, lroot, rroot, adam_row,
    fin, left_out, right_out, rows,
    xr, slots, zr, whole, lall, lsel, lhalf, rall, rsel, rwhole,
    mixed, precond, yr, back, xs, cols_t, lterm, rterm, norm,
    gx_send, gx_recv, gz_send, gz_recv, gy_send, gy_recv, gc_send, gc_recv,
    e_send, e_recv, l_send, l_recv, r_send, r_recv, f_send, f_recv,
    py_send, py_recv, pz_send, pz_recv, px_send, px_recv,
    dl_send, dl_recv, dr_send, dr_recv, df_send, df_recv, n_send, n_recv,
):
    x, y, z, c = position()
    entry_barrier(x, y, z, c)
    per_worker, rows_each, order = xr.shape
    width = order // NX
    half = order // NC
    sibling = (x, y, z, 1 - c)
    local = pltpu.make_async_copy

    def cols(index, size=width):
        return pl.ds(pl.multiple_of(index * size, size), size)

    def gx(k):
        to = (x + k) % NX
        return remote(send.at[to], xr.at[:, :, cols(x)], gx_send.at[k], gx_recv.at[k], (to, y, z, c))

    gx_own = local(send.at[x], xr.at[:, :, cols(x)], gx_recv.at[0])
    for k in RING:
        gx(k).start()
    gx_own.start()

    def exchange(s):
        return (
            remote(lroot.at[s, :, 1 - c], lall.at[NC * c + s], e_send.at[0, s], e_recv.at[0, s], sibling),
            remote(rroot.at[s, 1 - c], rall.at[NC * c + s], e_send.at[1, s], e_recv.at[1, s], sibling),
            local(lroot.at[s, :, c], lall.at[NC * c + s], e_recv.at[2, s]),
            local(rroot.at[s, c], rall.at[NC * c + s], e_recv.at[3, s]),
        )

    for s in range(2):
        for copy in exchange(s):
            copy.start()

    for k in RING:
        gx(k).wait_recv()
    gx_own.wait()

    def gz(m, k):
        to = (z + k) % NZ
        dst = whole.at[z, y, c] if m == 0 else zr.at[m, z]
        return remote(slots.at[m, to], dst, gz_send.at[m, k], gz_recv.at[m, k], (x, y, to, c))

    def gz_own(m):
        return local(slots.at[m, z], whole.at[z, y, c] if m == 0 else zr.at[m, z], gz_recv.at[m, 0])

    def gy(m):
        to = (y + m) % NY
        return remote(zr.at[m], whole.at[:, y, c], gy_send.at[m], gy_recv.at[m], (x, to, z, c))

    def gc(m):
        part = whole.at[:, (y - m + NY) % NY, c]
        return remote(part, part, gc_send.at[m], gc_recv.at[m], sibling)

    def build(m):
        to = (y + m) % NY

        def fill(i, carry):
            slots[m, i] = xr[table[i * NY + to]]
            return carry

        lax.fori_loop(0, NZ, fill, 0)
        for k in Z_ORDER:
            gz(m, k).start()
        gz_own(m).start()

    build(IN_ORDER[0])
    for s in range(2):
        a, b, d, e = exchange(s)
        a.wait_recv()
        b.wait_recv()
        d.wait()
        e.wait()

    def pick(i, carry):
        chosen = table[32 + i]
        lsel[i] = lall[chosen]
        rsel[i] = rall[chosen]
        return carry

    lax.fori_loop(0, NX, pick, 0)

    def lx(k):
        to = (x + k) % NX
        return remote(lsel.at[to], lhalf.at[x], l_send.at[k], l_recv.at[k], (to, y, z, c))

    def rx(k):
        to = (x + k) % NX
        return remote(rsel.at[to], rwhole.at[x, c], r_send.at[k], r_recv.at[k], (to, y, z, c))

    lx_own = local(lsel.at[x], lhalf.at[x], l_recv.at[0])
    rx_own = local(rsel.at[x], rwhole.at[x, c], r_recv.at[0])

    def forward(k):
        part = rwhole.at[(x - k + NX) % NX, c]
        return remote(part, part, f_send.at[k], f_recv.at[k], sibling)

    for k in RING:
        lx(k).start()
    lx_own.start()
    for k in RING:
        rx(k).start()
    rx_own.start()
    for m in IN_ORDER[1:]:
        build(m)

    def finish_y(m):
        gy(m).wait_recv()
        gc(m).start()

    rx_own.wait()
    forward(0).start()
    for i, m in enumerate(IN_ORDER):
        for k in Z_ORDER:
            gz(m, k).wait_recv()
        gz_own(m).wait()
        if m == 0:
            gc(0).start()
        else:
            gy(m).start()
        if i >= 1:
            finish_y(IN_ORDER[i - 1])
    for k in RING:
        rx(k).wait_recv()
        forward(k).start()
    for k in RING:
        lx(k).wait_recv()
    lx_own.wait()
    for m in IN_ORDER:
        gc(m).wait_recv()

    def dot(a, b, dims):
        return lax.dot_general(a, b, (dims, ((), ())), preferred_element_type=FULL)

    tiles = order // width

    def mix(n, carry):
        g = whole[:, :, :, :, cols(n)].reshape(order, width)
        mixed[:, cols(n)] = dot(lhalf[...].reshape(half, order), g, ((1,), (0,))).astype(LOW)
        return carry

    lax.fori_loop(0, tiles, mix, 0)
    for k in (0,) + RING:
        forward(k).wait_recv()

    def condition(n, carry):
        r = rwhole[:, :, :, cols(n)].reshape(order, width)
        p = dot(mixed[...], r, ((1,), (0,))).astype(LOW)
        precond[:, :, :, cols(n)] = p.reshape(NZ, NY, rows_each, width)
        wide = p.astype(FULL)
        return carry + jnp.sum(wide * wide, axis=0, keepdims=True)

    squares = lax.fori_loop(0, tiles, condition, jnp.zeros((1, width), FULL))

    def py(m):
        to = (y + m) % NY
        return remote(precond.at[:, to], yr.at[m], py_send.at[m], py_recv.at[m], (x, to, z, c))

    def pz(m, k):
        to = (z + k) % NZ
        src = precond.at[to, y] if m == 0 else yr.at[m, to]
        dst = back.at[z * NY + (y - m + NY) % NY]
        return remote(src, dst, pz_send.at[m, k], pz_recv.at[m, k], (x, y, to, c))

    def pz_own(m):
        src = precond.at[z, y] if m == 0 else yr.at[m, z]
        return local(src, back.at[z * NY + (y - m + NY) % NY], pz_recv.at[m, 0])

    def send_z(m):
        for k in Z_ORDER:
            pz(m, k).start()
        pz_own(m).start()

    def n_copies(stage):
        if stage == 0:
            part = rows.at[c, z, y, x]
            targets = [((x + k) % NX, y, z, c) for k in range(1, NX)]
        elif stage == 1:
            part = rows.at[c, z, y]
            targets = [(x, (y + k) % NY, z, c) for k in range(1, NY)]
        elif stage == 2:
            part = rows.at[c, z]
            targets = [(x, y, (z + k) % NZ, c) for k in range(1, NZ)]
        else:
            part = rows.at[c]
            targets = [sibling]
        return [
            remote(part, part, n_send.at[stage, i], n_recv.at[stage, i], target)
            for i, target in enumerate(targets)
        ]

    def n_step(stage):
        if stage > 0:
            for copy in n_copies(stage - 1):
                copy.wait_recv()
        if stage < 4:
            for copy in n_copies(stage):
                copy.start()

    for m in OUT_ORDER[1:]:
        py(m).start()
    send_z(0)
    norm[0:1, :] = adam_row[...]
    norm[1:2, :] = jnp.broadcast_to(jnp.sum(squares, axis=1, keepdims=True), (1, 128))
    n_own = local(norm, rows.at[c, z, y, x], n_recv.at[0, NZ - 1])
    n_own.start()
    n_own.wait()
    n_step(0)

    factor = 0.5 / order

    def gram_left(n, carry):
        own = whole[:, :, c].reshape(half, order)
        other = whole[pl.ds(n * NC, NC)].reshape(width, order)
        term = (factor * dot(own, other, ((1,), (1,)))).astype(LOW)
        lterm[:, :, :, cols(n)] = term.reshape(NX, half // (NX * rows_each), rows_each, width)
        return carry

    lax.fori_loop(0, tiles, gram_left, 0)

    def dlx(k):
        to = (x + k) % NX
        return remote(lterm.at[to], left_out.at[x, c], dl_send.at[k], dl_recv.at[k], (to, y, z, c))

    def drx(k):
        to = (x + k) % NX
        return remote(rterm.at[to], right_out.at[x, c], dr_send.at[k], dr_recv.at[k], (to, y, z, c))

    dl_own = local(lterm.at[x], left_out.at[x, c], dl_recv.at[0])
    dr_own = local(rterm.at[x], right_out.at[x, c], dr_recv.at[0])
    for k in RING:
        dlx(k).start()
    dl_own.start()
    py(OUT_ORDER[1]).wait_recv()
    send_z(OUT_ORDER[1])
    n_step(1)

    piece = width // NC

    def turn(i, carry):
        g = whole[:, :, :, :, cols(i * NC + c, piece)].reshape(order, piece)
        cols_t[pl.ds(pl.multiple_of(i * piece, piece), piece), :] = g.T
        return carry

    lax.fori_loop(0, NX, turn, 0)

    def gram_right(n, carry):
        g = whole[:, :, :, :, cols(n)].reshape(order, width)
        term = (factor * dot(cols_t[...], g, ((1,), (0,)))).astype(LOW)
        rterm[:, :, cols(n)] = term.reshape(NX, piece, width)
        return carry

    lax.fori_loop(0, tiles, gram_right, 0)
    for k in RING:
        drx(k).start()
    dr_own.start()
    for m in OUT_ORDER[2:]:
        py(m).wait_recv()
        send_z(m)
    n_step(2)

    def df(side, k):
        part = (left_out, right_out)[side].at[(x - k + NX) % NX, c]
        return remote(part, part, df_send.at[side, k], df_recv.at[side, k], sibling)

    dl_own.wait()
    df(0, 0).start()
    dr_own.wait()
    df(1, 0).start()
    for k in RING:
        dlx(k).wait_recv()
        df(0, k).start()
    n_step(3)
    for m in OUT_ORDER:
        for k in Z_ORDER:
            pz(m, k).wait_recv()
        pz_own(m).wait()

    def split(i, carry):
        rows_of = back[table[36 + i]]
        for t in range(NX):
            xs[t, i] = rows_of[:, t * width : (t + 1) * width]
        return carry

    lax.fori_loop(0, per_worker, split, 0)

    def px(k):
        to = (x + k) % NX
        return remote(xs.at[to], fin.at[x], px_send.at[k], px_recv.at[k], (to, y, z, c))

    px_own = local(xs.at[x], fin.at[x], px_recv.at[0])
    for k in RING:
        px(k).start()
    px_own.start()
    for k in RING:
        drx(k).wait_recv()
        df(1, k).start()
    n_step(4)
    px_own.wait()
    for k in RING:
        px(k).wait()
        gx(k).wait_send()
        lx(k).wait_send()
        rx(k).wait_send()
        gy(k).wait_send()
        py(k).wait_send()
        dlx(k).wait_send()
        drx(k).wait_send()
    for s in range(2):
        a, b, _, _ = exchange(s)
        a.wait_send()
        b.wait_send()
    for m in range(NY):
        for k in Z_ORDER:
            gz(m, k).wait_send()
            pz(m, k).wait_send()
        gc(m).wait_send()
        forward(m).wait_send()
        df(0, m).wait()
        df(1, m).wait()
    for stage in range(4):
        for copy in n_copies(stage):
            copy.wait_send()


def tail_kernel(
    table, place, flat, fin, rows, left_term, right_term, left_stat, right_stat,
    update, left_new, right_new, total,
):
    step = pl.program_id(0)
    blocks = update.shape[0]

    @pl.when(step == 0)
    def _():
        adam = jnp.sum(rows[:, 0:1, :], axis=0)
        total[...] = jnp.broadcast_to(adam, (128, 128)).T

    def apply(b, carry):
        index = step * blocks + b
        rank = place[index]
        worker = (flat[index] // NX) * NX + rank % NX
        root = rows[worker, 1:2, :] + rows[worker + NZ * NY * NX, 1:2, :]
        scale = jnp.sqrt(total[pl.ds(index, 1), :] / (root + 1e-06))
        wide = fin[rank % NX, rank // NX].astype(FULL)
        scale = jnp.concatenate([scale, scale], axis=1)
        update[b] = (wide * scale).astype(LOW)
        return carry

    lax.fori_loop(0, blocks, apply, 0)
    keep = jnp.where(table[48 + step // 4] > 0, 1, 0)
    for h in range(NC):
        term = jnp.where(keep > 0, left_term[0, h].astype(FULL), 0.0)
        left_new[0, :, h] = 0.5 * left_stat[0, :, h] + term
    right_new[0] = 0.5 * right_stat[0] + jnp.where(keep > 0, right_term[0].astype(FULL), 0.0)


ANY = pl.BlockSpec(memory_space=pl.ANY)
VMEM = pl.BlockSpec(memory_space=pltpu.VMEM)
DMA = pltpu.SemaphoreType.DMA


def tables(flat):
    x, y, z, c = position()
    rank = jnp.sum((flat[None, :] < flat[:, None]).astype(jnp.int32), axis=1)
    j = jnp.arange(64, dtype=jnp.int32)[:, None]
    f, r = flat[None, :], rank[None, :]
    chip = z * NY + y
    a = (f // 4 == j) & (r % NX == x)
    b = (f // 4 == chip) & (r % NX == j - 32)
    d = r == (j - 36) * NX + x
    e = f == (chip * NC + c) * 2 + j - 48
    value = jnp.where(
        j < 32,
        jnp.where(a, r // NX, 0),
        jnp.where(
            j < 36,
            jnp.where(b, f % 4, 0),
            jnp.where(j < 48, jnp.where(d, f // 4, 0), jnp.where(e & (j < 50), r % NX + 4, 0)),
        ),
    )
    return rank, jnp.sum(value, axis=1)


def per_device(
    gradient, second_moment, owner_table, slot_table, left_stat, right_stat, left_root, right_root
):
    blocks, rows, width = gradient.shape
    order = left_stat.shape[3]
    stripe = left_stat.shape[2]
    flat = owner_table * 2 + slot_table
    rank, table = tables(flat)
    each = blocks // NX
    groups = stripe // (NC * rows)
    shape = jax.ShapeDtypeStruct
    steps = 3
    block3 = pl.BlockSpec((blocks // steps, rows, width), lambda i, *_: (i, 0, 0))
    new_second, send, adam_row = pl.pallas_call(
        front_kernel,
        out_shape=(
            shape(gradient.shape, FULL),
            shape((NX, each, rows, width), LOW),
            shape((1, 128), FULL),
        ),
        grid_spec=pltpu.PrefetchScalarGridSpec(
            num_scalar_prefetch=1,
            grid=(steps,),
            in_specs=[block3, block3],
            out_specs=(
                block3,
                pl.BlockSpec((NX, each, rows, width), lambda i, *_: (0, 0, 0, 0)),
                pl.BlockSpec((1, 128), lambda i, *_: (0, 0)),
            ),
        ),
        name="front",
    )(rank, gradient, second_moment)

    half = order // NC
    fin, left_term, right_term, all_rows = pl.pallas_call(
        step_kernel,
        out_shape=(
            shape((NX, each, rows, width), LOW),
            shape((NX, NC, groups, rows, order), LOW),
            shape((NX, NC, stripe // NC, order), LOW),
            shape((NC, NZ, NY, NX, 2, 128), FULL),
        ),
        in_specs=[pl.BlockSpec(memory_space=pltpu.SMEM), ANY, ANY, ANY, VMEM],
        out_specs=(ANY,) * 4,
        scratch_shapes=[
            pltpu.VMEM((each, rows, order), LOW),
            pltpu.VMEM((NY, NZ, rows, order), LOW),
            pltpu.VMEM((NY, NZ, rows, order), LOW),
            pltpu.VMEM((NZ, NY, NC, rows, order), LOW),
            pltpu.VMEM((4, groups, rows, order), LOW),
            pltpu.VMEM((NX, groups, rows, order), LOW),
            pltpu.VMEM((NX, groups, rows, order), LOW),
            pltpu.VMEM((4, stripe // NC, order), LOW),
            pltpu.VMEM((NX, stripe // NC, order), LOW),
            pltpu.VMEM((NX, NC, stripe // NC, order), LOW),
            pltpu.VMEM((half, order), LOW),
            pltpu.VMEM((NZ, NY, rows, order), LOW),
            pltpu.VMEM((NY, NZ, rows, order), LOW),
            pltpu.VMEM((NZ * NY, rows, order), LOW),
            pltpu.VMEM((NX, each, rows, width), LOW),
            pltpu.VMEM((half, order), LOW),
            pltpu.VMEM((NX, groups, rows, order), LOW),
            pltpu.VMEM((NX, stripe // NC, order), LOW),
            pltpu.VMEM((2, 128), FULL),
            DMA((NX,)), DMA((NX,)), DMA((NY, NZ)), DMA((NY, NZ)),
            DMA((NY,)), DMA((NY,)), DMA((NY,)), DMA((NY,)),
            DMA((2, 2)), DMA((4, 2)), DMA((NX,)), DMA((NX,)), DMA((NX,)), DMA((NX,)),
            DMA((NX,)), DMA((NX,)),
            DMA((NY,)), DMA((NY,)), DMA((NY, NZ)), DMA((NY, NZ)), DMA((NX,)), DMA((NX,)),
            DMA((NX,)), DMA((NX,)), DMA((NX,)), DMA((NX,)), DMA((2, NX)), DMA((2, NX)),
            DMA((4, NZ)), DMA((4, NZ)),
        ],
        compiler_params=pltpu.CompilerParams(
            collective_id=0, has_side_effects=True, vmem_limit_bytes=48 << 20
        ),
        name="exchange_and_multiply",
    )(
        table,
        send,
        left_root.reshape(2, groups, NC, rows, order),
        right_root.reshape(2, NC, stripe // NC, order),
        adam_row,
    )

    steps = 8
    quarter = steps // 2
    part = blocks // steps

    def whole_spec(*dims):
        return pl.BlockSpec(dims, lambda i, *_: (0,) * len(dims))

    stat5 = pl.BlockSpec(
        (1, groups // quarter, NC, rows, order), lambda i, *_: (i // quarter, i % quarter, 0, 0, 0)
    )
    stat3 = pl.BlockSpec((1, stripe // quarter, order), lambda i, *_: (i // quarter, i % quarter, 0))
    update, left_new, right_new = pl.pallas_call(
        tail_kernel,
        out_shape=(
            shape(gradient.shape, LOW),
            shape((2, groups, NC, rows, order), FULL),
            shape((2, stripe, order), FULL),
        ),
        grid_spec=pltpu.PrefetchScalarGridSpec(
            num_scalar_prefetch=3,
            grid=(steps,),
            in_specs=[
                whole_spec(NX, each, rows, width),
                whole_spec(NC * NZ * NY * NX, 2, 128),
                pl.BlockSpec(
                    (1, NC, groups // quarter, rows, order),
                    lambda i, table, *_: (table[48 + i // quarter] % 4, 0, i % quarter, 0, 0),
                ),
                pl.BlockSpec(
                    (1, stripe // quarter, order),
                    lambda i, table, *_: (table[48 + i // quarter] % 4, i % quarter, 0),
                ),
                stat5,
                stat3,
            ],
            out_specs=(
                pl.BlockSpec((part, rows, width), lambda i, *_: (i, 0, 0)),
                stat5,
                stat3,
            ),
            scratch_shapes=[pltpu.VMEM((128, 128), FULL)],
        ),
        name="tail",
    )(
        table,
        rank,
        flat,
        fin,
        all_rows.reshape(NC * NZ * NY * NX, 2, 128),
        left_term,
        right_term.reshape(NX, stripe, order),
        left_stat.reshape(2, groups, NC, rows, order),
        right_stat.reshape(2, stripe, order),
    )
    return (
        update,
        new_second,
        left_new.reshape(left_stat.shape),
        right_new.reshape(right_stat.shape),
    )


def solution(mesh):
    placed = (
        P(None, "dp", "tensor"),
        P(None, "dp", "tensor"),
        P(),
        P(),
        P("dp", None, "tensor", None),
        P("dp", None, "tensor", None),
        P("dp", None, "tensor", None),
        P("dp", None, "tensor", None),
    )
    return jax.shard_map(
        per_device,
        mesh=mesh,
        in_specs=placed,
        out_specs=(
            P(None, "dp", "tensor"),
            P(None, "dp", "tensor"),
            P("dp", None, "tensor", None),
            P("dp", None, "tensor", None),
        ),
        check_vma=False,
    )
```

time: 298 us -> 109 us (0.37)
  waiting for transfers between devices: 129 us -> 0 us
  Pallas kernels: 0 us -> 101 us
  blocking collectives: 94 us -> 0 us
  starting transfers between devices: 21.8 us -> 0 us
  matrix products: 14.8 us -> 0 us
  between operations: 14.2 us -> 0.78 us
  local copies, waits for them, and re-layouts: 18.6 us -> 5.98 us
  other arithmetic: 4.19 us -> 1.13 us
    pallas_call x0 -> x3, Pallas kernels: none -> 101 us  [the longest x1 87 us: per_device(): pl.pallas_call(step_kernel, out_shape=(shape((NX, each, rows, width), LOW...]
    all_to_all x2 -> x0, waiting for transfers between devices: 94 us -> none  [the longest x1 94 us: per_device(): lax.all_to_all(buffer, 'dp', split_axis=0, concat_axis=1, tiled=True)]
    psum x1 -> x0, blocking collectives: 77.7 us -> none  [per_device(): adam_total, root_total = lax.psum((adam_part, root_part), ('dp', 'tensor'))]
    all_gather x2 -> x0, waiting for transfers between devices: 34.7 us -> none  [the longest x1 34.7 us: per_device(): gathered = lax.all_gather(grad_low, 'tensor', axis=2, tiled=True)]
    all_to_all x2 -> x0, starting transfers between devices: 21.7 us -> none  [the longest x1 12.2 us: per_device(): lax.all_to_all(buffer, 'dp', split_axis=0, concat_axis=1, tiled=True)]
    all_to_all x1 -> x0, blocking collectives: 16.3 us -> none  [per_device(): lax.all_to_all(precond, 'tensor', split_axis=2, concat_axis=1, tiled=True)]
    dot_general x3 -> x0, matrix products: 14.8 us -> none  [the longest x1 6.14 us: per_device(): jnp.einsum('sik,skj->sij', mixed, lax.all_gather(right_root[0], 'tensor',...]
    all_to_all x6 -> x0, local copies, waits for them, and re-layouts: 7.95 us -> none  [the longest x1 4.98 us: per_device(): lax.all_to_all(buffer, 'dp', split_axis=0, concat_axis=1, tiled=True)]
  transfers between devices with their start and end apart: 4 -> 0, of which waited for: 2 -> 0; matrix products, arithmetic and copies ran while one was open for 5% -> 0% of each run, Pallas kernels for 0% -> 0%
where the time goes in v2:
time: 109 us; the launch traced here: 108 us
  Pallas kernels  101 us (93%)
  local copies, waits for them, and re-layouts  5.98 us (5%)
  other arithmetic  1.13 us (1%)
    pallas_call x1, Pallas kernels, per_device(): pl.pallas_call(step_kernel, out_shape=(shape((NX, each, rows, width), LOW...  87 us
    pallas_call x1, Pallas kernels, per_device(): pl.pallas_call(tail_kernel, out_shape=(shape(gradient.shape, LOW), shape(...  9.33 us
    unnamed x20, local copies, waits for them, and re-layouts  5.98 us
    pallas_call x1, Pallas kernels, per_device(): pl.pallas_call(front_kernel, out_shape=(shape(gradient.shape, FULL), shap...  4.24 us

profile of v2, /device:TPU:1, one launch (start us, length us, event | category | flops | bytes accessed | tf_op | source)
XLA Modules:
  0.0 108.5 jit_solution(2911900177235620044)
XLA Ops:
  0.6 0.0 copy-start.1
  0.7 0.8 broadcast_compare_fusion
  1.5 0.0 copy-start.9
  1.5 0.2 convert_reduce_fusion.rank.place
  1.7 0.0 copy-start.8
  1.7 0.1 select_reduce_fusion.table
  1.9 0.3 copy-done.8
  2.2 0.0 copy-start.6
  2.2 4.2 %front.1 = (f32[48,16,256]{2,1,0:T(8,128)}, bf16[4,12,16,256]{3,2,1,0:T(8,128)(2,1)}, f32[1,128]{1,0:T(1,128)}) custom-call(s32[48]{0:T(128)} %copy-done.8, f32[48,16,256]{2,1,0:T(8,128)} %gradient.1, f32[48,16,256]{2,1,0:T(8,128)} %second_moment.1), custom_call_target="tpu_custom_call" | custom-call | tf_op jit(solution)/shard_map/front/pallas_call | solution.py:481
  6.4 0.0 copy-done.1
  6.4 0.0 copy-start.2
  6.5 1.2 %copy-done.2 = bf16[1,2,256,1024]{3,2,1,0:T(8,128)(2,1)S(1)} copy-done((bf16[1,2,256,1024]{3,2,1,0:T(8,128)(2,1)S(1)}, bf16[1,2,256,1024]{3,2,1,0:T(8,128)(2,1)}, u32[]{:S(2)}) %copy-start.2) | copy-done | bytes 1048600
  7.7 0.0 copy-start.4
  7.7 1.0 copy-done.4
  8.7 0.0 copy-start.7
  8.7 0.7 copy-done.7
  9.3 87.0 %exchange_and_multiply.1 = (bf16[4,12,16,256]{3,2,1,0:T(8,128)(2,1)S(1)}, bf16[4,2,8,16,1024]{4,3,2,1,0:T(8,128)(2,1)S(1)}, bf16[4,2,128,1024]{3,2,1,0:T(8,128)(2,1)}, f32[2,8,4,4,2,128]{5,4,3,2,1,0:T(2,128)S(1)}) custom-call(s32[64]{0:T(128)S(1)} %select_reduce_fusion.table, bf16[4,12,16,256]{3,2,1,0:T(8,128)(2,1)S(1)} %copy-done.4, ...), custom_call_target="tpu_custom_call" | custom-call | tf_op jit(solution)/shard_map/exchange_and_multiply/pallas_call | solution.py:502
  96.3 0.0 copy-start
  96.3 1.3 %copy-done = bf16[4,2,8,16,1024]{4,3,2,1,0:T(8,128)(2,1)} copy-done((bf16[4,2,8,16,1024]{4,3,2,1,0:T(8,128)(2,1)}, bf16[4,2,8,16,1024]{4,3,2,1,0:T(8,128)(2,1)S(1)}, u32[]{:S(2)}) %copy-start) | copy-done | bytes 2097176
  97.6 0.0 copy-start.3
  97.6 0.8 copy-done.3
  98.4 0.0 copy-start.5
  98.4 0.7 copy-done.5
  99.1 0.0 copy-done.9
  99.1 0.0 copy-done.6
  99.1 9.3 %tail.1 = (bf16[48,16,256]{2,1,0:T(8,128)(2,1)}, f32[2,8,2,16,1024]{4,3,2,1,0:T(8,128)}, f32[2,256,1024]{2,1,0:T(8,128)}) custom-call(s32[64]{0:T(128)} %copy-done.6, s32[48]{0:T(128)} %copy-done.8, s32[48]{0:T(128)} %copy-done.9, bf16[4,12,16,256]{3,2,1,0:T(8,128)(2,1)} %copy-done.3, f32[256,2,128]{2,1,0:T(2,128)} %bitcast.10, ...), custom_call_target="tpu_custom_call" | custom-call | tf_op jit(solution)/shard_map/tail/pallas_call | solution.py:563
  (7 shorter events, 0.1 us)
Async XLA Ops:
  0.6 5.8 %copy-start.1 = (bf16[1,2,256,1024]{3,2,1,0:T(8,128)(2,1)S(1)}, bf16[1,2,256,1024]{3,2,1,0:T(8,128)(2,1)}, u32[]{:S(2)}) copy-start(bf16[1,2,256,1024]{3,2,1,0:T(8,128)(2,1)} %param.14) | copy-start | bytes 3145732
  1.5 97.6 %copy-start.9 = (s32[48]{0:T(128)}, s32[48]{0:T(128)S(1)}, u32[]{:S(2)}) copy-start(s32[48]{0:T(128)S(1)} %get-tuple-element.28.flat) | copy-start | bytes 580
  1.7 0.5 copy-start.8
  2.2 96.9 %copy-start.6 = (s32[64]{0:T(128)}, s32[64]{0:T(128)S(1)}, u32[]{:S(2)}) copy-start(s32[64]{0:T(128)S(1)} %select_reduce_fusion.table) | copy-start | bytes 772
  6.4 1.2 %copy-start.2 = (bf16[1,2,256,1024]{3,2,1,0:T(8,128)(2,1)S(1)}, bf16[1,2,256,1024]{3,2,1,0:T(8,128)(2,1)}, u32[]{:S(2)}) copy-start(bf16[1,2,256,1024]{3,2,1,0:T(8,128)(2,1)} %param.15) | copy-start | bytes 3145732
  7.7 1.0 copy-start.4
  8.7 0.7 copy-start.7
  96.3 1.3 %copy-start = (bf16[4,2,8,16,1024]{4,3,2,1,0:T(8,128)(2,1)}, bf16[4,2,8,16,1024]{4,3,2,1,0:T(8,128)(2,1)S(1)}, u32[]{:S(2)}) copy-start(bf16[4,2,8,16,1024]{4,3,2,1,0:T(8,128)(2,1)S(1)} %get-tuple-element.18.left_term) | copy-start | bytes 6291460
  97.6 0.8 copy-start.3
  98.4 0.7 copy-start.5
